TPU v7x, 512 devices: a whole 4x8x8 slice. The times are simulated.
512 devices in a mesh: tensor: 8 (over x, core), context: 64 (over z, y).
Axes of the slice: x: 4, y: 8, z: 8, core: 2. Of those that a mesh axis runs over, the one named last changes fastest.
Arguments:
- token_ids: int32 [2, 6144], P(None, 'context'), may hold values from 0 to 151935
- embed_table: bfloat16 [4096, 151936], P('context', 'tensor')
- input_gain: float32 [4096], replicated, may hold values from 0.1 to 1.9
- w_qkv: bfloat16 [4096, 6144], P('context', 'tensor')
- q_gain: float32 [128], replicated, may hold values from 1 to 10
- k_gain: float32 [128], replicated, may hold values from 1 to 10
Outputs:
- attended: bfloat16 [64, 6144, 128], P('context', 'tensor')
All inputs are finite; a program needn't handle non-finite values.
Results may differ from a plain program's by a relative error of at most 0.0085.
The roundings to bfloat16 on the way count: a program that leaves them out, or rounds other values in their place, can miss the bound.
Values may be sent and summed in bfloat16 or wider, within the bound.
A program may use at most 64 MiB of HBM per device.

v0:
```python
import math
import jax
import jax.numpy as jnp
from jax import lax
from jax.sharding import PartitionSpec as P

QH = 32
KVH = 8
HD = 128
ROPE_BASE = 1000000.0
EPSILON = 1e-06
NEGATIVE = -1e30


def rope_tables(positions, width):
    half_width = width // 2
    exponent = jnp.arange(half_width, dtype=jnp.float32) * (2.0 / width)
    inverse = jnp.exp(-exponent * jnp.log(jnp.float32(ROPE_BASE)))
    angles = positions.astype(jnp.float32)[:, None] * inverse[None, :]
    angles = jnp.concatenate([angles, angles], axis=-1)
    return (jnp.cos(angles), jnp.sin(angles))


def norm_rope(head_vals, head_gain, cos_table, sin_table):
    mean_sq = jnp.mean(head_vals * head_vals, axis=-1, keepdims=True)
    scaled = head_vals * lax.rsqrt(mean_sq + EPSILON) * head_gain
    half_width = scaled.shape[-1] // 2
    rotated = jnp.concatenate([-scaled[..., half_width:], scaled[..., :half_width]], axis=-1)
    return scaled * cos_table[:, None, :] + rotated * sin_table[:, None, :]


def feature_norm(embedded, input_gain):
    hidden = embedded.astype(jnp.float32)
    mean_sq = jnp.mean(hidden * hidden, axis=0, keepdims=True)
    return (hidden * lax.rsqrt(mean_sq + EPSILON) * input_gain[:, None, None]).astype(jnp.bfloat16)


def shards(token_ids, embed_table, input_gain, w_qkv, q_gain, k_gain):
    tensor_count = lax.axis_size("tensor")
    tensor_rank = lax.axis_index("tensor")
    context_rank = lax.axis_index("context")
    seq_count, local_len = token_ids.shape
    width_part, vocab_part = embed_table.shape
    all_ids = lax.all_gather(token_ids, "context", axis=1, tiled=True)
    full_len = all_ids.shape[1]
    local_ids = all_ids - tensor_rank * vocab_part
    inside = (local_ids >= 0) & (local_ids < vocab_part)
    picked = jnp.take(embed_table, jnp.clip(local_ids, 0, vocab_part - 1), axis=1)
    partial_rows = jnp.where(inside[None], picked.astype(jnp.float32), 0.0)
    summed = lax.psum(partial_rows.astype(jnp.bfloat16), "tensor")
    embedded = lax.all_to_all(summed, "context", split_axis=2, concat_axis=0, tiled=True)
    normed = feature_norm(embedded, input_gain)
    projected = jnp.einsum(
        "dsl,dk->slk",
        normed,
        lax.all_gather(w_qkv, "context", axis=0, tiled=True),
        preferred_element_type=jnp.float32,
    )
    joined_proj = lax.all_gather(projected.astype(jnp.bfloat16), "tensor", axis=2, tiled=True)
    positions = context_rank * local_len + jnp.arange(local_len, dtype=jnp.int32)
    cos_table, sin_table = rope_tables(positions, HD)
    wide = joined_proj.astype(jnp.float32)
    queries = norm_rope(
        wide[..., : QH * HD].reshape(seq_count, local_len, QH, HD), q_gain, cos_table, sin_table
    ).astype(jnp.bfloat16)
    key_heads = norm_rope(
        wide[..., QH * HD : (QH + KVH) * HD].reshape(seq_count, local_len, KVH, HD),
        k_gain,
        cos_table,
        sin_table,
    ).astype(jnp.bfloat16)
    values = joined_proj[..., (QH + KVH) * HD :].reshape(seq_count, local_len, KVH, HD)
    group_size = QH // KVH
    queries = jnp.transpose(queries, (0, 2, 1, 3)).reshape(seq_count * QH, local_len, HD)
    key_heads = jnp.repeat(jnp.transpose(key_heads, (0, 2, 1, 3)), group_size, axis=1).reshape(
        seq_count * QH, local_len, HD
    )
    values = jnp.repeat(jnp.transpose(values, (0, 2, 1, 3)), group_size, axis=1).reshape(
        seq_count * QH, local_len, HD
    )
    queries, key_heads, values = (
        lax.all_to_all(queries, "context", split_axis=0, concat_axis=1, tiled=True),
        lax.all_to_all(key_heads, "context", split_axis=0, concat_axis=1, tiled=True),
        lax.all_to_all(values, "context", split_axis=0, concat_axis=1, tiled=True),
    )
    unit_count = queries.shape[0]
    block_rows = full_len // tensor_count
    own_queries = lax.dynamic_slice_in_dim(queries, tensor_rank * block_rows, block_rows, 1)
    query_pos = tensor_rank * block_rows + jnp.arange(block_rows, dtype=jnp.int32)
    query_block = math.gcd(block_rows, 512)
    query_steps = block_rows // query_block
    key_block = math.gcd(full_len, 512)
    key_steps = full_len // key_block
    key_tiles = key_heads.reshape(unit_count, key_steps, key_block, HD)
    value_tiles = values.reshape(unit_count, key_steps, key_block, HD)
    score_scale = HD ** (-0.5)
    outputs = []
    for q_index in range(query_steps):
        query_tile = own_queries[:, q_index * query_block : (q_index + 1) * query_block]
        block_pos = query_pos[q_index * query_block : (q_index + 1) * query_block]
        last_pos = jnp.max(block_pos)

        def key_step(key_index, state_now):
            key_start = key_index * key_block

            def attend(state_in):
                old_max, old_total, old_acc = state_in
                key_tile = lax.dynamic_index_in_dim(key_tiles, key_index, 1, keepdims=False)
                value_tile = lax.dynamic_index_in_dim(value_tiles, key_index, 1, keepdims=False)
                scores = (
                    jnp.einsum(
                        "uqd,ukd->uqk", query_tile, key_tile, preferred_element_type=jnp.float32
                    )
                    * score_scale
                )
                key_pos = key_start + jnp.arange(key_block, dtype=jnp.int32)
                allowed = (key_pos[None, :] <= block_pos[:, None])[None]
                scores = jnp.where(allowed, scores, NEGATIVE)
                new_max = jnp.maximum(old_max, jnp.max(scores, axis=-1))
                weights = jnp.where(allowed, jnp.exp(scores - new_max[..., None]), 0.0)
                shrink = jnp.exp(old_max - new_max)
                new_total = old_total * shrink + jnp.sum(weights, axis=-1)
                new_acc = old_acc * shrink[..., None] + jnp.einsum(
                    "uqk,ukd->uqd",
                    weights.astype(jnp.bfloat16),
                    value_tile,
                    preferred_element_type=jnp.float32,
                )
                return (new_max, new_total, new_acc)

            return lax.cond(key_start <= last_pos, attend, lambda unchanged: unchanged, state_now)

        starting = (
            jnp.full((unit_count, query_block), NEGATIVE, jnp.float32),
            jnp.zeros((unit_count, query_block), jnp.float32),
            jnp.zeros((unit_count, query_block, HD), jnp.float32),
        )
        run_max, run_total, run_acc = lax.fori_loop(0, key_steps, key_step, starting)
        outputs.append((run_acc / run_total[..., None]).astype(jnp.bfloat16))
    attended = jnp.concatenate(outputs, axis=1)
    return attended


def solution(mesh):
    return jax.shard_map(
        shards,
        mesh=mesh,
        in_specs=(
            P(None, "context"),
            P("context", "tensor"),
            P(),
            P("context", "tensor"),
            P(),
            P(),
        ),
        out_specs=P("context", "tensor", None),
        check_vma=False,
    )
```

profile of v0, /device:TPU:15, one launch (start us, length us, event | category | flops | bytes accessed | tf_op | source)
XLA Modules:
  0.0 587.6 jit_solution(8688220472509900719)
XLA Ops:
  7.4 43.1 %all-gather = s32[64,96,2]{1,2,0:T(2,128)S(1)} all-gather(s32[1,96,2]{1,2,0:T(2,128)} %bitcast.203), channel_id=1, replica_groups=mesh['tensor'=8,'context'=64] {'context'}, dimensions={0}, use_global_device_ids=true | all-gather | bytes 49920 | tf_op jit(solution)/shard_map/all_gather | solution.py:44
  50.8 5.8 copy.85
  60.4 35.7 %gather_fusion = bf16[12288,64]{1,0:T(8,128)(2,1)S(1)} fusion(bf16[64,18992]{0,1:T(8,128)(2,1)} %copy.85, s32[12288]{0:T(1024)S(1)} %broadcast_clamp_fusion), kind=kCustom, calls=%fused_computation | custom fusion | bytes 3194880 | tf_op jit(solution)/shard_map/jit(_take)/gather | solution.py:48
  96.1 29.7 %fusion.58 = bf16[64,2,6144]{0,1,2:T(2,128)(2,1)} fusion(pred[2,6144]{0,1:T(8,128)(4,1)} %copy.84, pred[2,6144]{0,1:T(8,128)(4,1)} %copy.83, bf16[2,6144,64]{2,1,0:T(8,128)(2,1)S(1)} %bitcast.176), kind=kLoop, calls=%fused_computation.77 | loop fusion | flops 3145728 | bytes 3170304 | tf_op jit(solution)/shard_map/convert_element_type | solution.py:50
  126.3 89.1 %all-reduce.2.cloned.1.call-done = bf16[64,2,6144]{0,1,2:T(2,128)(2,1)} async-done(((bf16[64,2,6144]{0,1,2:T(2,128)(2,1)}), bf16[64,2,6144]{0,1,2:T(2,128)(2,1)}) %all-reduce.2.cloned.1.call-update) | async-done | bytes 1572880 | tf_op jit(solution)/shard_map/psum | solution.py:50
  215.4 7.8 %reshape.275 = bf16[64,2,6144]{2,1,0:T(2,128)(2,1)} reshape(bf16[6144,2,64]{2,1,0:T(2,128)(2,1)} %bitcast.179) | data formatting | bytes 3145728
  223.2 12.8 %all-to-all-start = ((bf16[64,2,6144]{2,1,0:T(2,128)(2,1)}), bf16[64,2,6144]{2,1,0:T(2,128)(2,1)S(1)}, u32[]{:S(2)}, u32[]{:S(2)}) async-start(bf16[64,2,6144]{2,1,0:T(2,128)(2,1)} %reshape.275), calls=%async_computation | async-start | bytes 3145728 | tf_op jit(solution)/shard_map/all_to_all | solution.py:51
  236.3 40.8 %all-to-all-done = bf16[64,2,6144]{2,1,0:T(2,128)(2,1)S(1)} async-done(((bf16[64,2,6144]{2,1,0:T(2,128)(2,1)}), bf16[64,2,6144]{2,1,0:T(2,128)(2,1)S(1)}, u32[]{:S(2)}, u32[]{:S(2)}) %all-to-all-start) | async-done | bytes 1572896 | tf_op jit(solution)/shard_map/all_to_all | solution.py:51
  277.1 3.4 reshape.276
  280.5 6.3 %copy.87 = bf16[64,2,6144]{2,0,1:T(8,128)(2,1)S(1)} copy(bf16[64,2,6144]{0,1,2:T(2,128)(2,1)} %bitcast.169) | data formatting | bytes 3145728 | tf_op jit(solution)/shard_map/all_to_all | solution.py:51
  286.8 3.2 reshape.251
  290.1 6.7 %copy.88 = f32[64,64,2,96]{3,1,0,2:T(8,128)} copy(f32[64,64,2,96]{3,0,1,2:T(8,128)} %bitcast.168) | data formatting | bytes 6291456 | tf_op jit(solution)/shard_map/convert_element_type | solution.py:33
  301.2 4.9 fusion.63
  306.5 26.0 %all-gather.6.cloned.1.call-done = bf16[2,96,6144]{2,1,0:T(8,128)(2,1)} async-done(((bf16[2,96,768]{2,1,0:T(8,128)(2,1)}), bf16[2,96,6144]{2,1,0:T(8,128)(2,1)}) %all-gather.6.cloned.1.call-update) | async-done | bytes 2359312 | tf_op jit(solution)/shard_map/all_gather | solution.py:59
  339.3 3.0 fusion.62
  342.3 13.1 %all-to-all-start.2 = ((bf16[64,96,128]{2,1,0:T(8,128)(2,1)}), bf16[64,96,128]{2,1,0:T(8,128)(2,1)}, u32[]{:S(2)}, u32[]{:S(2)}) async-start(bf16[64,96,128]{2,1,0:T(8,128)(2,1)} %bitcast.178), calls=%async_computation.2 | async-start | bytes 3145728 | tf_op jit(solution)/shard_map/all_to_all | solution.py:82
  357.2 38.0 %all-to-all-done.2 = bf16[64,96,128]{2,1,0:T(8,128)(2,1)} async-done(((bf16[64,96,128]{2,1,0:T(8,128)(2,1)}), bf16[64,96,128]{2,1,0:T(8,128)(2,1)}, u32[]{:S(2)}, u32[]{:S(2)}) %all-to-all-start.2) | async-done | bytes 1572896 | tf_op jit(solution)/shard_map/all_to_all | solution.py:82
  396.6 8.3 %all-to-all-start.1 = ((bf16[64,96,128]{2,1,0:T(8,128)(2,1)}), bf16[64,96,128]{2,1,0:T(8,128)(2,1)}, u32[]{:S(2)}, u32[]{:S(2)}) async-start(bf16[64,96,128]{2,1,0:T(8,128)(2,1)} %bitcast.177), calls=%async_computation.1 | async-start | bytes 3145728 | tf_op jit(solution)/shard_map/all_to_all | solution.py:83
  405.1 38.4 %all-to-all-done.1 = bf16[64,96,128]{2,1,0:T(8,128)(2,1)} async-done(((bf16[64,96,128]{2,1,0:T(8,128)(2,1)}), bf16[64,96,128]{2,1,0:T(8,128)(2,1)}, u32[]{:S(2)}, u32[]{:S(2)}) %all-to-all-start.1) | async-done | bytes 1572896 | tf_op jit(solution)/shard_map/all_to_all | solution.py:83
  444.9 7.4 %all-to-all-start.3 = ((bf16[64,96,128]{2,1,0:T(8,128)(2,1)}), bf16[64,96,128]{2,1,0:T(8,128)(2,1)S(1)}, u32[]{:S(2)}, u32[]{:S(2)}) async-start(bf16[64,96,128]{2,1,0:T(8,128)(2,1)} %bitcast.44), calls=%async_computation.3 | async-start | bytes 3145728 | tf_op jit(solution)/shard_map/all_to_all | solution.py:84
  453.9 36.7 %all-to-all-done.3 = bf16[64,96,128]{2,1,0:T(8,128)(2,1)S(1)} async-done(((bf16[64,96,128]{2,1,0:T(8,128)(2,1)}), bf16[64,96,128]{2,1,0:T(8,128)(2,1)S(1)}, u32[]{:S(2)}, u32[]{:S(2)}) %all-to-all-start.3) | async-done | bytes 1572896 | tf_op jit(solution)/shard_map/all_to_all | solution.py:84
  490.6 28.7 %while.51 = (s32[]{:T(128)}, f32[1,256]{1,0:T(1,128)S(1)}, f32[1,256]{1,0:T(1,128)S(1)}, f32[1,256,128]{2,1,0:T(8,128)S(1)}, s32[]{:T(128)}, /*index=5*/s32[256]...) while((s32[]{:T(128)}, f32[1,256]{1,0:T(1,128)S(1)}, ...), condition=%wide.region_11.12_spmd, body=%wide.region_6.11_spmd.sunk | while | flops 68748288 | bytes 2190645 | solution.py:138
  519.3 30.0 %while.52 = (s32[]{:T(128)}, f32[1,256]{1,0:T(1,128)S(1)}, f32[1,256]{1,0:T(1,128)S(1)}, f32[1,256,128]{2,1,0:T(8,128)S(1)}, s32[]{:T(128)}, /*index=5*/s32[256]...) while((s32[]{:T(128)}, f32[1,256]{1,0:T(1,128)S(1)}, ...), condition=%wide.region_18.19_spmd, body=%wide.region_13.18_spmd.sunk | while | flops 68748288 | bytes 2190645 | solution.py:138
  549.3 29.9 %while.53 = (s32[]{:T(128)}, f32[1,256]{1,0:T(1,128)S(1)}, f32[1,256]{1,0:T(1,128)S(1)}, f32[1,256,128]{2,1,0:T(8,128)S(1)}, s32[]{:T(128)}, /*index=5*/s32[256]...) while((s32[]{:T(128)}, f32[1,256]{1,0:T(1,128)S(1)}, ...), condition=%wide.region_25.26_spmd, body=%wide.region_20.25_spmd.sunk | while | flops 68748288 | bytes 2190645 | solution.py:138
  (356 shorter events, 151.0 us)
Async XLA Ops:
  7.4 208.0 %all-reduce.2.cloned.1.call-start = ((), (), s32[]{:S(2)}) async-start(), calls=%async_computation.4 | async-start | bytes 6291456 | tf_op jit(solution)/shard_map/psum | solution.py:50
  125.7 175.4 %all-gather.4.cloned.1.call-start = ((), (), s32[]{:S(2)}) async-start(), calls=%async_computation.5 | async-start | bytes 6389760 | tf_op jit(solution)/shard_map/all_gather | solution.py:56
  223.2 53.9 %all-to-all-start = ((bf16[64,2,6144]{2,1,0:T(2,128)(2,1)}), bf16[64,2,6144]{2,1,0:T(2,128)(2,1)S(1)}, u32[]{:S(2)}, u32[]{:S(2)}) async-start(bf16[64,2,6144]{2,1,0:T(2,128)(2,1)} %reshape.275), calls=%async_computation | async-start | bytes 3145728 | tf_op jit(solution)/shard_map/all_to_all | solution.py:51
  236.0 96.5 %all-gather.6.cloned.1.call-start = ((), (), s32[]{:S(2)}) async-start(), calls=%async_computation.6 | async-start | bytes 2654208 | tf_op jit(solution)/shard_map/all_gather | solution.py:59
  297.1 1.4 copy-start.1
  334.8 1.7 copy-start
  336.5 0.7 copy-start.2
  342.3 13.8 %copy-start.3 = (f32[128]{0:T(128)S(1)}, f32[128]{0:T(128)}, u32[]{:S(2)}) copy-start(f32[128]{0:T(128)} %param.23) | copy-start | bytes 1540
  342.3 52.9 %all-to-all-start.2 = ((bf16[64,96,128]{2,1,0:T(8,128)(2,1)}), bf16[64,96,128]{2,1,0:T(8,128)(2,1)}, u32[]{:S(2)}, u32[]{:S(2)}) async-start(bf16[64,96,128]{2,1,0:T(8,128)(2,1)} %bitcast.178), calls=%async_computation.2 | async-start | bytes 3145728 | tf_op jit(solution)/shard_map/all_to_all | solution.py:82
  357.2 47.7 %slice-start = ((bf16[2,96,6144]{2,1,0:T(8,128)(2,1)}), bf16[2,96,1024]{2,1,0:T(8,128)(2,1)S(1)}, s32[]{:S(2)}) async-start(bf16[2,96,6144]{2,1,0:T(8,128)(2,1)} %all-gather.6.cloned.1.call-done), calls=%async_computation.7 | async-start | bytes 786432 | tf_op jit(solution)/shard_map/slice | solution.py:72
  396.6 46.9 %all-to-all-start.1 = ((bf16[64,96,128]{2,1,0:T(8,128)(2,1)}), bf16[64,96,128]{2,1,0:T(8,128)(2,1)}, u32[]{:S(2)}, u32[]{:S(2)}) async-start(bf16[64,96,128]{2,1,0:T(8,128)(2,1)} %bitcast.177), calls=%async_computation.1 | async-start | bytes 3145728 | tf_op jit(solution)/shard_map/all_to_all | solution.py:83
  444.9 45.7 %all-to-all-start.3 = ((bf16[64,96,128]{2,1,0:T(8,128)(2,1)}), bf16[64,96,128]{2,1,0:T(8,128)(2,1)S(1)}, u32[]{:S(2)}, u32[]{:S(2)}) async-start(bf16[64,96,128]{2,1,0:T(8,128)(2,1)} %bitcast.44), calls=%async_computation.3 | async-start | bytes 3145728 | tf_op jit(solution)/shard_map/all_to_all | solution.py:84
Sparse Core Ops, SparseCore 0:
  125.9 89.5 all-reduce.1
  306.3 26.2 all-gather.5
Sparse Core Ops, SparseCore 1:
  129.2 96.6 all-gather.3
where the time goes:
time: 590 us; the launch traced here: 588 us
  waiting for transfers between devices  270 us (46%)
  local copies, waits for them, and re-layouts  81.6 us (14%)
  matrix products  61.3 us (10%)
  other arithmetic  49.3 us (8%)
  blocking collectives  43.1 us (7%)
  starting transfers between devices  41.8 us (7%)
  loops' own time  25.6 us (4%)
  between operations  15.3 us (3%)
    psum x1, waiting for transfers between devices, shards(): summed = lax.psum(partial_rows.astype(jnp.bfloat16), 'tensor')  89.1 us
    all_gather x1, blocking collectives, shards(): all_ids = lax.all_gather(token_ids, 'context', axis=1, tiled=True)  43.1 us
    dot_general x35, matrix products, attend(): jnp.einsum('uqd,ukd->uqk', query_tile, key_tile, preferred_element_type=j...  41.2 us
    all_to_all x1, waiting for transfers between devices, shards(): lax.all_to_all(summed, 'context', split_axis=2, concat_axis=0, tiled=True)  40.8 us
    all_to_all x1, waiting for transfers between devices, shards(): lax.all_to_all(key_heads, 'context', split_axis=0, concat_axis=1, tiled=T...  38.4 us
    all_to_all x1, waiting for transfers between devices, shards(): lax.all_to_all(queries, 'context', split_axis=0, concat_axis=1, tiled=True)  38 us
    all_to_all x1, waiting for transfers between devices, shards(): lax.all_to_all(values, 'context', split_axis=0, concat_axis=1, tiled=True)  36.7 us
    gather x1, local copies, waits for them, and re-layouts, shards(): jnp.take(embed_table, jnp.clip(local_ids, 0, vocab_part - 1), axis=1)  35.7 us
  transfers between devices with their start and end apart: 7, of which 6 were waited for; matrix products, arithmetic and copies ran while one was open for 6% of the time, Pallas kernels for 0%

commit v1 on v0

--- a/solution.py
+++ b/solution.py
@@ -41,7 +41,8 @@
     context_rank = lax.axis_index("context")
     seq_count, local_len = token_ids.shape
     width_part, vocab_part = embed_table.shape
-    all_ids = lax.all_gather(token_ids, "context", axis=1, tiled=True)
+    sent = jnp.stack([token_ids] * lax.axis_size("context"))
+    all_ids = jnp.concatenate(lax.all_to_all(sent, "context", 0, 0), axis=1)
     full_len = all_ids.shape[1]
     local_ids = all_ids - tensor_rank * vocab_part
     inside = (local_ids >= 0) & (local_ids < vocab_part)

time: 590 us -> 556 us (0.942)
  blocking collectives: 43.1 us -> 0 us
  starting transfers between devices: 41.8 us -> 57.9 us
  waiting for transfers between devices: 270 us -> 262 us
    all_gather x1 -> x0, blocking collectives: 43.1 us -> none  [shards(): all_ids = lax.all_gather(token_ids, 'context', axis=1, tiled=True)]
    all_to_all x0 -> x1, starting transfers between devices: none -> 16 us  [shards(): all_ids = jnp.concatenate(lax.all_to_all(sent, 'context', 0, 0), axis=1)]
    psum x1, waiting for transfers between devices: 89.1 us -> 76.9 us  [shards(): summed = lax.psum(partial_rows.astype(jnp.bfloat16), 'tensor')]
  transfers between devices with their start and end apart: 7 -> 8, of which waited for: 6 -> 7; matrix products, arithmetic and copies ran while one was open for 6% -> 7% of each run, Pallas kernels for 0% -> 0%
where the time goes in v1:
time: 556 us; the launch traced here: 554 us
  waiting for transfers between devices  262 us (47%)
  local copies, waits for them, and re-layouts  82.9 us (15%)
  matrix products  61.3 us (11%)
  starting transfers between devices  57.9 us (10%)
  other arithmetic  49.3 us (9%)
  loops' own time  24.8 us (4%)
  between operations  15.3 us (3%)
    psum x1, waiting for transfers between devices, shards(): summed = lax.psum(partial_rows.astype(jnp.bfloat16), 'tensor')  76.9 us
    dot_general x35, matrix products, attend(): jnp.einsum('uqd,ukd->uqk', query_tile, key_tile, preferred_element_type=j...  41.2 us
    all_to_all x1, waiting for transfers between devices, shards(): lax.all_to_all(summed, 'context', split_axis=2, concat_axis=0, tiled=True)  40.8 us
    all_to_all x1, waiting for transfers between devices, shards(): lax.all_to_all(key_heads, 'context', split_axis=0, concat_axis=1, tiled=T...  38.4 us
    all_to_all x1, waiting for transfers between devices, shards(): lax.all_to_all(queries, 'context', split_axis=0, concat_axis=1, tiled=True)  38 us
    all_to_all x1, waiting for transfers between devices, shards(): lax.all_to_all(values, 'context', split_axis=0, concat_axis=1, tiled=True)  36.7 us
    gather x1, local copies, waits for them, and re-layouts, shards(): jnp.take(embed_table, jnp.clip(local_ids, 0, vocab_part - 1), axis=1)  35.7 us
    convert_element_type x1, other arithmetic, shards(): summed = lax.psum(partial_rows.astype(jnp.bfloat16), 'tensor')  29.7 us
  transfers between devices with their start and end apart: 8, of which 7 were waited for; matrix products, arithmetic and copies ran while one was open for 7% of the time, Pallas kernels for 0%

profile of v1, /device:TPU:15, one launch (start us, length us, event | category | flops | bytes accessed | tf_op | source)
XLA Modules:
  0.0 553.6 jit_solution(7496762003331523830)
XLA Ops:
  8.7 16.0 %all-to-all-start = ((s32[64,2,96]{2,1,0:T(2,128)}), s32[64,2,96]{2,1,0:T(2,128)S(1)}, u32[]{:S(2)}, u32[]{:S(2)}) async-start(s32[64,2,96]{2,1,0:T(2,128)} %stack.2), calls=%async_computation | async-start | bytes 131072 | tf_op jit(solution)/shard_map/all_to_all | solution.py:45
  24.8 5.8 %copy.97 = bf16[64,18992]{0,1:T(8,128)(2,1)} copy(bf16[64,18992]{1,0:T(8,128)(2,1)} %param.19) | data formatting | bytes 4861952 | tf_op args[1]
  30.6 4.7 all-to-all-done
  39.5 35.7 %gather_fusion = bf16[12288,64]{1,0:T(8,128)(2,1)S(1)} fusion(bf16[64,18992]{0,1:T(8,128)(2,1)} %copy.97, s32[12288]{0:T(1024)S(1)} %broadcast_clamp_fusion), kind=kCustom, calls=%fused_computation | custom fusion | bytes 3194880 | tf_op jit(solution)/shard_map/jit(_take)/gather | solution.py:49
  75.2 29.7 %fusion.58 = bf16[64,2,6144]{0,1,2:T(2,128)(2,1)} fusion(pred[2,6144]{0,1:T(8,128)(4,1)} %copy.95, pred[2,6144]{0,1:T(8,128)(4,1)} %bitcast.173, bf16[2,6144,64]{2,1,0:T(8,128)(2,1)S(1)} %bitcast.168), kind=kLoop, calls=%fused_computation.77 | loop fusion | flops 3145728 | bytes 3170304 | tf_op jit(solution)/shard_map/convert_element_type | solution.py:51
  105.4 76.9 %all-reduce.2.cloned.1.call-done = bf16[64,2,6144]{0,1,2:T(2,128)(2,1)} async-done(((bf16[64,2,6144]{0,1,2:T(2,128)(2,1)}), bf16[64,2,6144]{0,1,2:T(2,128)(2,1)}) %all-reduce.2.cloned.1.call-update) | async-done | bytes 1572880 | tf_op jit(solution)/shard_map/psum | solution.py:51
  182.3 7.8 %reshape.311 = bf16[64,2,6144]{2,1,0:T(2,128)(2,1)} reshape(bf16[6144,2,64]{2,1,0:T(2,128)(2,1)} %bitcast.171) | data formatting | bytes 3145728
  190.2 12.8 %all-to-all-start.1 = ((bf16[64,2,6144]{2,1,0:T(2,128)(2,1)}), bf16[64,2,6144]{2,1,0:T(2,128)(2,1)S(1)}, u32[]{:S(2)}, u32[]{:S(2)}) async-start(bf16[64,2,6144]{2,1,0:T(2,128)(2,1)} %reshape.311), calls=%async_computation.1 | async-start | bytes 3145728 | tf_op jit(solution)/shard_map/all_to_all | solution.py:52
  203.2 40.8 %all-to-all-done.1 = bf16[64,2,6144]{2,1,0:T(2,128)(2,1)S(1)} async-done(((bf16[64,2,6144]{2,1,0:T(2,128)(2,1)}), bf16[64,2,6144]{2,1,0:T(2,128)(2,1)S(1)}, u32[]{:S(2)}, u32[]{:S(2)}) %all-to-all-start.1) | async-done | bytes 1572896 | tf_op jit(solution)/shard_map/all_to_all | solution.py:52
  244.0 3.4 reshape.312
  247.4 6.3 %copy.99 = bf16[64,2,6144]{2,0,1:T(8,128)(2,1)S(1)} copy(bf16[64,2,6144]{0,1,2:T(2,128)(2,1)} %bitcast.161) | data formatting | bytes 3145728 | tf_op jit(solution)/shard_map/all_to_all | solution.py:52
  253.7 3.2 reshape.300
  256.9 6.7 %copy.100 = f32[64,64,2,96]{3,1,0,2:T(8,128)} copy(f32[64,64,2,96]{3,0,1,2:T(8,128)} %bitcast.160) | data formatting | bytes 6291456 | tf_op jit(solution)/shard_map/convert_element_type | solution.py:33
  268.1 4.9 fusion.63
  273.4 25.9 %all-gather.5.cloned.1.call-done = bf16[2,96,6144]{2,1,0:T(8,128)(2,1)} async-done(((bf16[2,96,768]{2,1,0:T(8,128)(2,1)}), bf16[2,96,6144]{2,1,0:T(8,128)(2,1)}) %all-gather.5.cloned.1.call-update) | async-done | bytes 2359312 | tf_op jit(solution)/shard_map/all_gather | solution.py:60
  309.1 13.1 %all-to-all-start.3 = ((bf16[64,96,128]{2,1,0:T(8,128)(2,1)}), bf16[64,96,128]{2,1,0:T(8,128)(2,1)}, u32[]{:S(2)}, u32[]{:S(2)}) async-start(bf16[64,96,128]{2,1,0:T(8,128)(2,1)} %bitcast.170), calls=%async_computation.3 | async-start | bytes 3145728 | tf_op jit(solution)/shard_map/all_to_all | solution.py:83
  324.1 38.0 %all-to-all-done.3 = bf16[64,96,128]{2,1,0:T(8,128)(2,1)} async-done(((bf16[64,96,128]{2,1,0:T(8,128)(2,1)}), bf16[64,96,128]{2,1,0:T(8,128)(2,1)}, u32[]{:S(2)}, u32[]{:S(2)}) %all-to-all-start.3) | async-done | bytes 1572896 | tf_op jit(solution)/shard_map/all_to_all | solution.py:83
  363.4 8.3 %all-to-all-start.2 = ((bf16[64,96,128]{2,1,0:T(8,128)(2,1)}), bf16[64,96,128]{2,1,0:T(8,128)(2,1)}, u32[]{:S(2)}, u32[]{:S(2)}) async-start(bf16[64,96,128]{2,1,0:T(8,128)(2,1)} %bitcast.169), calls=%async_computation.2 | async-start | bytes 3145728 | tf_op jit(solution)/shard_map/all_to_all | solution.py:84
  371.9 38.4 %all-to-all-done.2 = bf16[64,96,128]{2,1,0:T(8,128)(2,1)} async-done(((bf16[64,96,128]{2,1,0:T(8,128)(2,1)}), bf16[64,96,128]{2,1,0:T(8,128)(2,1)}, u32[]{:S(2)}, u32[]{:S(2)}) %all-to-all-start.2) | async-done | bytes 1572896 | tf_op jit(solution)/shard_map/all_to_all | solution.py:84
  411.7 7.4 %all-to-all-start.4 = ((bf16[64,96,128]{2,1,0:T(8,128)(2,1)}), bf16[64,96,128]{2,1,0:T(8,128)(2,1)S(1)}, u32[]{:S(2)}, u32[]{:S(2)}) async-start(bf16[64,96,128]{2,1,0:T(8,128)(2,1)} %bitcast.43), calls=%async_computation.4 | async-start | bytes 3145728 | tf_op jit(solution)/shard_map/all_to_all | solution.py:85
  420.7 36.7 %all-to-all-done.4 = bf16[64,96,128]{2,1,0:T(8,128)(2,1)S(1)} async-done(((bf16[64,96,128]{2,1,0:T(8,128)(2,1)}), bf16[64,96,128]{2,1,0:T(8,128)(2,1)S(1)}, u32[]{:S(2)}, u32[]{:S(2)}) %all-to-all-start.4) | async-done | bytes 1572896 | tf_op jit(solution)/shard_map/all_to_all | solution.py:85
  457.4 27.1 %while.51 = (s32[]{:T(128)}, f32[1,256]{1,0:T(1,128)S(1)}, f32[1,256]{1,0:T(1,128)S(1)}, f32[1,256,128]{2,1,0:T(8,128)S(1)}, s32[]{:T(128)}, /*index=5*/s32[256]...) while((s32[]{:T(128)}, f32[1,256]{1,0:T(1,128)S(1)}, ...), condition=%wide.region_11.12_spmd, body=%wide.region_6.11_spmd.sunk | while | flops 68748288 | bytes 2190645 | solution.py:139
  484.6 30.5 %while.52 = (s32[]{:T(128)}, f32[1,256]{1,0:T(1,128)S(1)}, f32[1,256]{1,0:T(1,128)S(1)}, f32[1,256,128]{2,1,0:T(8,128)S(1)}, s32[]{:T(128)}, /*index=5*/s32[256]...) while((s32[]{:T(128)}, f32[1,256]{1,0:T(1,128)S(1)}, ...), condition=%wide.region_18.19_spmd, body=%wide.region_13.18_spmd.sunk | while | flops 68748288 | bytes 2190645 | solution.py:139
  515.1 30.0 %while.53 = (s32[]{:T(128)}, f32[1,256]{1,0:T(1,128)S(1)}, f32[1,256]{1,0:T(1,128)S(1)}, f32[1,256,128]{2,1,0:T(8,128)S(1)}, s32[]{:T(128)}, /*index=5*/s32[256]...) while((s32[]{:T(128)}, f32[1,256]{1,0:T(1,128)S(1)}, ...), condition=%wide.region_25.26_spmd, body=%wide.region_20.25_spmd.sunk | while | flops 68748288 | bytes 2190645 | solution.py:139
  (359 shorter events, 155.4 us)
Async XLA Ops:
  8.7 26.6 %all-to-all-start = ((s32[64,2,96]{2,1,0:T(2,128)}), s32[64,2,96]{2,1,0:T(2,128)S(1)}, u32[]{:S(2)}, u32[]{:S(2)}) async-start(s32[64,2,96]{2,1,0:T(2,128)} %stack.2), calls=%async_computation | async-start | bytes 131072 | tf_op jit(solution)/shard_map/all_to_all | solution.py:45
  24.7 157.6 %all-reduce.2.cloned.1.call-start = ((), (), s32[]{:S(2)}) async-start(), calls=%async_computation.5 | async-start | bytes 6291456 | tf_op jit(solution)/shard_map/psum | solution.py:51
  104.8 163.2 %all-gather.3.cloned.1.call-start = ((), (), s32[]{:S(2)}) async-start(), calls=%async_computation.6 | async-start | bytes 6389760 | tf_op jit(solution)/shard_map/all_gather | solution.py:57
  190.2 53.9 %all-to-all-start.1 = ((bf16[64,2,6144]{2,1,0:T(2,128)(2,1)}), bf16[64,2,6144]{2,1,0:T(2,128)(2,1)S(1)}, u32[]{:S(2)}, u32[]{:S(2)}) async-start(bf16[64,2,6144]{2,1,0:T(2,128)(2,1)} %reshape.311), calls=%async_computation.1 | async-start | bytes 3145728 | tf_op jit(solution)/shard_map/all_to_all | solution.py:52
  203.0 96.4 %all-gather.5.cloned.1.call-start = ((), (), s32[]{:S(2)}) async-start(), calls=%async_computation.7 | async-start | bytes 2654208 | tf_op jit(solution)/shard_map/all_gather | solution.py:60
  264.0 1.4 copy-start.1
  301.6 1.7 copy-start
  303.3 0.7 copy-start.2
  309.1 13.8 %copy-start.3 = (f32[128]{0:T(128)S(1)}, f32[128]{0:T(128)}, u32[]{:S(2)}) copy-start(f32[128]{0:T(128)} %param.23) | copy-start | bytes 1540
  309.1 52.9 %all-to-all-start.3 = ((bf16[64,96,128]{2,1,0:T(8,128)(2,1)}), bf16[64,96,128]{2,1,0:T(8,128)(2,1)}, u32[]{:S(2)}, u32[]{:S(2)}) async-start(bf16[64,96,128]{2,1,0:T(8,128)(2,1)} %bitcast.170), calls=%async_computation.3 | async-start | bytes 3145728 | tf_op jit(solution)/shard_map/all_to_all | solution.py:83
  324.1 47.7 %slice-start = ((bf16[2,96,6144]{2,1,0:T(8,128)(2,1)}), bf16[2,96,1024]{2,1,0:T(8,128)(2,1)S(1)}, s32[]{:S(2)}) async-start(bf16[2,96,6144]{2,1,0:T(8,128)(2,1)} %all-gather.5.cloned.1.call-done), calls=%async_computation.8 | async-start | bytes 786432 | tf_op jit(solution)/shard_map/slice | solution.py:73
  363.4 46.9 %all-to-all-start.2 = ((bf16[64,96,128]{2,1,0:T(8,128)(2,1)}), bf16[64,96,128]{2,1,0:T(8,128)(2,1)}, u32[]{:S(2)}, u32[]{:S(2)}) async-start(bf16[64,96,128]{2,1,0:T(8,128)(2,1)} %bitcast.169), calls=%async_computation.2 | async-start | bytes 3145728 | tf_op jit(solution)/shard_map/all_to_all | solution.py:84
  411.7 45.7 %all-to-all-start.4 = ((bf16[64,96,128]{2,1,0:T(8,128)(2,1)}), bf16[64,96,128]{2,1,0:T(8,128)(2,1)S(1)}, u32[]{:S(2)}, u32[]{:S(2)}) async-start(bf16[64,96,128]{2,1,0:T(8,128)(2,1)} %bitcast.43), calls=%async_computation.4 | async-start | bytes 3145728 | tf_op jit(solution)/shard_map/all_to_all | solution.py:85
Sparse Core Ops, SparseCore 0:
  105.0 77.3 all-reduce.1
  273.1 26.1 all-gather.4
Sparse Core Ops, SparseCore 1:
  108.3 84.4 all-gather.2
